TPU v7x, 32 devices: a whole 2x2x4 slice. The times are simulated.
32 devices in a mesh: face: 4 (over x, core), tile: 8 (over z, y).
Axes of the slice: x: 2, y: 2, z: 4, core: 2. Of those that a mesh axis runs over, the one named last changes fastest.
Arguments:
- field_in: bfloat16 [12, 48, 256, 256], P('face', None, 'tile'), may hold values from -6 to 6
- out_grad: bfloat16 [12, 48, 256, 256], P('face', None, 'tile'), may hold values from -6 to 6
- weight_first: bfloat16 [48, 48, 3, 3], replicated, may hold values from -0.3125 to 0.3125
- bias_first: float32 [48], replicated, may hold values from -3 to 3
- weight_second: bfloat16 [48, 48, 3, 3], replicated, may hold values from -0.3125 to 0.3125
- bias_second: float32 [48], replicated, may hold values from -3 to 3
- face_links: int32 [12, 4, 3], replicated, may hold values from 0 to 11, as said below
- corner_rules: int32 [12, 4], replicated, may hold values from 0 to 1
Outputs:
- output_field: bfloat16 [12, 48, 256, 256], P('face', None, 'tile')
- grad_field: bfloat16 [12, 48, 256, 256], P('face', None, 'tile')
- grad_weight_first: float32 [48, 48, 3, 3], replicated
- grad_bias_first: float32 [48], replicated
- grad_weight_second: float32 [48, 48, 3, 3], replicated
- grad_bias_second: float32 [48], replicated
Inputs may be any that keep to these rules, and one draw needn't show every extreme that they name: face_links[f, e] = (g, e2, r) glues edge e of face f to edge e2 of face g; r = 1 when positions along the two edges run in opposite directions. The gluing is a pairing: (g, e2) differs from (f, e) and face_links[g, e2] = (f, e, r). The partner face lies in 0..11, the edge in 0..3, the flag in 0..1.
All inputs are finite; a program needn't handle non-finite values.
Results may differ from a plain program's by a relative error of at most 0.0055.
The roundings to bfloat16 on the way count: a program that leaves them out, or rounds other values in their place, can miss the bound.
Values may be sent and summed in bfloat16 or wider, within the bound.
A program may use at most 256 MiB of HBM per device.

v0:
```python
import jax
import jax.numpy as jnp
from jax import lax
from jax.sharding import PartitionSpec as P

INV_ROOT_TWO = 0.7071067811865476
INV_ROOT_TWO_PI = 0.3989422804014327


def shortened(x):
    return jax.tree.map(lambda a: a.astype(jnp.bfloat16) if a.dtype == jnp.float32 else a, x)


def extended_2(block, sides, width):
    for axis, dim in sides:
        count = lax.axis_size(axis)
        forward = [(i, i + 1) for i in range(count - 1)]
        backward = [(target, source) for source, target in forward]
        low = lax.ppermute(
            lax.slice_in_dim(block, block.shape[dim] - width, None, axis=dim), axis, forward
        )
        high = lax.ppermute(lax.slice_in_dim(block, 0, width, axis=dim), axis, backward)
        block = jnp.concatenate([low, block, high], axis=dim)
    return block


def gelu_pair(values):
    normal_cdf = 0.5 * (1.0 + lax.erf(values * INV_ROOT_TWO))
    normal_pdf = jnp.exp(-0.5 * values * values) * INV_ROOT_TWO_PI
    return (values * normal_cdf, normal_cdf + values * normal_pdf)


def convolve(padded, weight):
    return lax.conv_general_dilated(
        padded,
        weight,
        (1, 1),
        "VALID",
        dimension_numbers=("NCHW", "OIHW", "NCHW"),
        preferred_element_type=jnp.float32,
    )


def halo_rows(strip):
    return extended_2(shortened(strip), (("tile", 2),), 1).astype(strip.dtype)


def place_lines(north_row, south_row, west_part, east_part, tile_pos, tile_count):
    seg_len = west_part.shape[-1]
    mirrored = tile_count - 1 - tile_pos
    blanks = jnp.zeros(north_row.shape, jnp.float32)
    north_full = jnp.where(tile_pos == 0, north_row.astype(jnp.float32), blanks)
    south_full = jnp.where(tile_pos == tile_count - 1, south_row.astype(jnp.float32), blanks)
    west_wide = west_part.astype(jnp.float32)
    east_wide = east_part.astype(jnp.float32)
    west_full = lax.dynamic_update_slice_in_dim(blanks, west_wide, tile_pos * seg_len, 2)
    east_full = lax.dynamic_update_slice_in_dim(blanks, east_wide, tile_pos * seg_len, 2)
    placed = jnp.stack([north_full, south_full, west_full, east_full], axis=1)
    own_lines = lax.psum(placed.astype(jnp.bfloat16), "tile")
    front = lax.dynamic_slice_in_dim(own_lines, tile_pos * seg_len, seg_len, 3)
    back = lax.dynamic_slice_in_dim(own_lines, mirrored * seg_len, seg_len, 3)
    return (front, back)


def partner_pieces(front, my_links, tile_pos, tile_count):
    faces_dev, _, channels, seg_len = front.shape
    side_len = seg_len * tile_count
    partner_face = my_links[:, :, 0].reshape(-1)
    partner_edge = my_links[:, :, 1].reshape(-1)
    flip_mask = (my_links[:, :, 2] == 1).reshape(-1)
    gathered = lax.all_gather(front, ("face", "tile"), axis=3, tiled=True)

    def fetch_line(face_id, edge_id):
        start = (face_id % faces_dev, edge_id, 0, face_id // faces_dev * side_len)
        return lax.dynamic_slice(gathered, start, (1, 1, channels, side_len))[0, 0]

    source = jax.vmap(fetch_line)(partner_face, partner_edge)
    ghosts = jnp.where(flip_mask[:, None, None], source[:, :, ::-1], source)
    ghosts = ghosts.reshape(faces_dev, 4, channels, side_len)
    north_row = ghosts[:, 0]
    south_row = ghosts[:, 1]
    west_part = lax.dynamic_slice_in_dim(ghosts[:, 2], tile_pos * seg_len, seg_len, 2)
    east_part = lax.dynamic_slice_in_dim(ghosts[:, 3], tile_pos * seg_len, seg_len, 2)
    return (north_row, south_row, west_part, east_part)


def fill_strip(activation, my_links, my_corners, tile_pos, tile_count):
    front, back = place_lines(
        activation[:, :, 0, :],
        activation[:, :, -1, :],
        activation[:, :, :, 0],
        activation[:, :, :, -1],
        tile_pos,
        tile_count,
    )
    north_row, south_row, west_part, east_part = partner_pieces(
        front, my_links, tile_pos, tile_count
    )
    corner_code = (my_corners == 0)[:, :, None]
    corner_nw = jnp.where(corner_code[:, 0], north_row[:, :, 0], west_part[:, :, 0])
    corner_ne = jnp.where(corner_code[:, 1], north_row[:, :, -1], east_part[:, :, 0])
    corner_sw = jnp.where(corner_code[:, 2], south_row[:, :, 0], west_part[:, :, -1])
    corner_se = jnp.where(corner_code[:, 3], south_row[:, :, -1], east_part[:, :, -1])
    middle = jnp.concatenate(
        [west_part[:, :, :, None], activation, east_part[:, :, :, None]], axis=3
    )
    extended = halo_rows(middle)
    top_row = jnp.concatenate([corner_nw[:, :, None], north_row, corner_ne[:, :, None]], axis=2)
    bottom_row = jnp.concatenate([corner_sw[:, :, None], south_row, corner_se[:, :, None]], axis=2)
    top_rim = jnp.where(tile_pos == 0, top_row, extended[:, :, 0])
    bottom_rim = jnp.where(tile_pos == tile_count - 1, bottom_row, extended[:, :, -1])
    return jnp.concatenate(
        [top_rim[:, :, None], extended[:, :, 1:-1], bottom_rim[:, :, None]], axis=2
    )


def unfold_strip(cotangent, weight, my_links, my_corners, tile_pos, tile_count):
    widened = jnp.pad(cotangent, ((0, 0), (0, 0), (0, 0), (1, 1)))
    extended = halo_rows(widened)
    padded = jnp.pad(extended, ((0, 0), (0, 0), (1, 1), (1, 1)))
    flipped = jnp.transpose(weight[:, :, ::-1, ::-1], (1, 0, 2, 3))
    pad_grad = convolve(padded, flipped)
    at_top = tile_pos == 0
    at_bottom = tile_pos == tile_count - 1
    north_row = pad_grad[:, :, 0, 1:-1]
    south_row = pad_grad[:, :, -1, 1:-1]
    west_part = pad_grad[:, :, 1:-1, 0]
    east_part = pad_grad[:, :, 1:-1, -1]
    corner_nw = pad_grad[:, :, 0, 0]
    corner_ne = pad_grad[:, :, 0, -1]
    corner_sw = pad_grad[:, :, -1, 0]
    corner_se = pad_grad[:, :, -1, -1]
    corner_code = my_corners[:, :, None]
    north_row = north_row.at[:, :, 0].add(jnp.where(corner_code[:, 0] == 0, corner_nw, 0.0))
    north_row = north_row.at[:, :, -1].add(jnp.where(corner_code[:, 1] == 0, corner_ne, 0.0))
    south_row = south_row.at[:, :, 0].add(jnp.where(corner_code[:, 2] == 0, corner_sw, 0.0))
    south_row = south_row.at[:, :, -1].add(jnp.where(corner_code[:, 3] == 0, corner_se, 0.0))
    west_part = west_part.at[:, :, 0].add(
        jnp.where((corner_code[:, 0] == 1) & at_top, corner_nw, 0.0)
    )
    west_part = west_part.at[:, :, -1].add(
        jnp.where((corner_code[:, 2] == 1) & at_bottom, corner_sw, 0.0)
    )
    east_part = east_part.at[:, :, 0].add(
        jnp.where((corner_code[:, 1] == 1) & at_top, corner_ne, 0.0)
    )
    east_part = east_part.at[:, :, -1].add(
        jnp.where((corner_code[:, 3] == 1) & at_bottom, corner_se, 0.0)
    )
    front, back = place_lines(
        north_row.astype(jnp.bfloat16),
        south_row.astype(jnp.bfloat16),
        west_part.astype(jnp.bfloat16),
        east_part.astype(jnp.bfloat16),
        tile_pos,
        tile_count,
    )
    back_north, back_south, back_west, back_east = partner_pieces(
        front, my_links, tile_pos, tile_count
    )
    interior = pad_grad[:, :, 1:-1, 1:-1]
    interior = interior.at[:, :, 0, :].add(jnp.where(at_top, back_north.astype(jnp.float32), 0.0))
    interior = interior.at[:, :, -1, :].add(
        jnp.where(at_bottom, back_south.astype(jnp.float32), 0.0)
    )
    interior = interior.at[:, :, :, 0].add(back_west.astype(jnp.float32))
    interior = interior.at[:, :, :, -1].add(back_east.astype(jnp.float32))
    return interior


def weight_grad(cotangent, padded):
    return lax.conv_general_dilated(
        padded,
        cotangent,
        (1, 1),
        "VALID",
        dimension_numbers=("CNHW", "IOHW", "CNHW"),
        preferred_element_type=jnp.float32,
    )


def body(
    field_in,
    out_grad,
    weight_first,
    bias_first,
    weight_second,
    bias_second,
    face_links,
    corner_rules,
):
    tile_count = lax.axis_size("tile")
    tile_pos = lax.axis_index("tile")
    face_pos = lax.axis_index("face")
    faces_dev = field_in.shape[0]
    side_len = field_in.shape[3]
    my_links = lax.dynamic_slice_in_dim(face_links, face_pos * faces_dev, faces_dev, 0)
    my_corners = lax.dynamic_slice_in_dim(corner_rules, face_pos * faces_dev, faces_dev, 0)
    padded_first = fill_strip(field_in, my_links, my_corners, tile_pos, tile_count)
    pre_first = convolve(padded_first, weight_first) + bias_first[None, :, None, None]
    gelu_first, slope_first = gelu_pair(pre_first)
    hidden = gelu_first.astype(jnp.bfloat16)
    padded_second = fill_strip(hidden, my_links, my_corners, tile_pos, tile_count)
    pre_second = convolve(padded_second, weight_second) + bias_second[None, :, None, None]
    gelu_second, slope_second = gelu_pair(pre_second)
    output_field = gelu_second.astype(jnp.bfloat16)
    grad_second = (out_grad.astype(jnp.float32) * slope_second).astype(jnp.bfloat16)
    weight_second_part = weight_grad(grad_second, padded_second)
    bias_second_part = jnp.sum(grad_second.astype(jnp.float32), axis=(0, 2, 3))
    grad_hidden = unfold_strip(
        grad_second, weight_second, my_links, my_corners, tile_pos, tile_count
    )
    grad_first = (grad_hidden * slope_first).astype(jnp.bfloat16)
    weight_first_part = weight_grad(grad_first, padded_first)
    bias_first_part = jnp.sum(grad_first.astype(jnp.float32), axis=(0, 2, 3))
    grad_field = unfold_strip(
        grad_first, weight_first, my_links, my_corners, tile_pos, tile_count
    ).astype(jnp.bfloat16)
    totals = lax.psum(
        (weight_first_part, bias_first_part, weight_second_part, bias_second_part), ("face", "tile")
    )
    return (
        output_field,
        grad_field,
        totals[0] / side_len,
        totals[1] / side_len,
        totals[2] / side_len,
        totals[3] / side_len,
    )


def solution(mesh):
    return jax.shard_map(
        body,
        mesh=mesh,
        in_specs=(
            P("face", None, "tile", None),
            P("face", None, "tile", None),
            P(),
            P(),
            P(),
            P(),
            P(),
            P(),
        ),
        out_specs=(
            P("face", None, "tile", None),
            P("face", None, "tile", None),
            P(),
            P(),
            P(),
            P(),
        ),
        check_vma=False,
    )
```

profile of v0, /device:TPU:0, one launch (start us, length us, event | category | flops | bytes accessed | tf_op | source)
XLA Modules:
  0.0 1963.4 jit_solution(1567796698921269111)
XLA Ops:
  19.2 74.5 %all-reduce.10.cloned.1.call-done = bf16[3,4,48,256]{3,2,0,1:T(8,128)(2,1)} async-done(((bf16[3,4,48,256]{3,2,0,1:T(8,128)(2,1)}), bf16[3,4,48,256]{3,2,0,1:T(8,128)(2,1)}) %all-reduce.10.cloned.1.call-update) | async-done | bytes 294928 | tf_op jit(solution)/shard_map/psum | solution.py:59
  103.9 51.9 %all-gather.5.cloned.1.call-done = bf16[3,4,48,1024]{2,1,0,3:T(4,128)(2,1)} async-done(((bf16[3,4,48,32]{2,1,0,3:T(4,128)(2,1)}), bf16[3,4,48,1024]{2,1,0,3:T(4,128)(2,1)}) %all-gather.5.cloned.1.call-update) | async-done | bytes 1179664 | tf_op jit(solution)/shard_map/all_gather | solution.py:71
  179.5 17.8 fusion.87
  203.9 24.2 %copy.2867 = bf16[48,34,3,8,33]{4,3,0,2,1:T(8,128)(2,1)} copy(bf16[48,34,3,8,33]{0,2,4,3,1:T(4,128)(2,1)} %bitcast.324) | data formatting | bytes 5170176 | tf_op jit(solution)/shard_map/conv_general_dilated | solution.py:34
  239.8 15.0 fusion.13
  254.8 14.0 copy.2762
  268.8 23.4 %fusion.8 = (f32[32,24,33,48]{3,1,2,0:T(8,128)}, bf16[32,24,33,48]{3,1,2,0:T(8,128)(2,1)S(1)}) fusion(f32[48]{0:T(128)S(1)} %copy-done.49, pred[24,33]{0,1:T(8,128)(4,1)S(1)} %copy-done.53, bf16[48,48,3,3]{1,0,3,2:T(8,128)(2,1)S(1)} %copy-done.47, bf16[48,34,3,8,35]{0,3,2,4,1:T(8,128)(2,1)} %copy.2762), kind=kOutput, calls=%fused_computation.21 | convolution fusion | flops 1065664512 | bytes 10083288 | tf_op jit(solution)/shard_map/conv_general_dilated | solution.py:34
  311.7 72.1 %all-reduce.12.cloned.1.call-done = bf16[3,4,48,256]{3,2,0,1:T(8,128)(2,1)} async-done(((bf16[3,4,48,256]{3,2,0,1:T(8,128)(2,1)}), bf16[3,4,48,256]{3,2,0,1:T(8,128)(2,1)}) %all-reduce.12.cloned.1.call-update) | async-done | bytes 294928 | tf_op jit(solution)/shard_map/psum | solution.py:59
  386.0 59.4 %all-gather.7.cloned.1.call-done = bf16[3,4,48,1024]{2,1,0,3:T(4,128)(2,1)} async-done(((bf16[3,4,48,32]{2,1,0,3:T(4,128)(2,1)}), bf16[3,4,48,1024]{2,1,0,3:T(4,128)(2,1)}) %all-gather.7.cloned.1.call-update) | async-done | bytes 1179664 | tf_op jit(solution)/shard_map/all_gather | solution.py:71
  468.6 19.1 fusion.84
  494.3 24.2 %copy.2872 = bf16[48,34,3,8,33]{4,3,0,2,1:T(8,128)(2,1)} copy(bf16[48,34,3,8,33]{0,2,4,3,1:T(4,128)(2,1)} %bitcast.325) | data formatting | bytes 5170176 | tf_op jit(solution)/shard_map/conv_general_dilated | solution.py:34
  530.2 15.0 fusion.14
  545.2 14.0 copy.2782
  559.2 22.5 %fusion.12 = (f32[32,24,33,48]{3,1,2,0:T(8,128)}, bf16[32,24,33,48]{3,1,2,0:T(8,128)(2,1)}) fusion(f32[48]{0:T(128)S(1)} %copy-done.50, pred[24,33]{0,1:T(8,128)(4,1)S(1)} %copy-done.53, bf16[48,48,3,3]{1,0,3,2:T(8,128)(2,1)S(1)} %copy-done, bf16[48,34,3,8,35]{0,3,2,4,1:T(8,128)(2,1)} %copy.2782), kind=kOutput, calls=%fused_computation.25 | convolution fusion | flops 1065664512 | bytes 10083288 | tf_op jit(solution)/shard_map/conv_general_dilated | solution.py:34
  639.9 14.1 reshape.1719
  665.8 15.0 fusion.15
  680.7 14.0 copy.2790
  694.7 22.0 %convolution_select_fusion.1 = f32[34,24,33,48]{3,1,2,0:T(8,128)} fusion(bf16[48,48,3,3]{1,0,3,2:T(8,128)(2,1)S(1)} %copy-done, bf16[48,34,3,8,35]{0,3,2,4,1:T(8,128)(2,1)} %copy.2790, pred[24,33]{0,1:T(8,128)(4,1)S(1)} %copy-done.51), kind=kOutput, calls=%fused_computation.37 | convolution fusion | flops 1096153344 | bytes 7954200 | tf_op jit(solution)/shard_map/conv_general_dilated | solution.py:34
  716.7 13.6 copy.2791
  730.3 15.7 reshape.1723
  746.0 17.6 copy.2888
  763.6 29.2 %fusion.67 = (f32[3,48,1,256]{2,1,0,3:T(8,128)}, f32[3,48,1,256]{2,1,0,3:T(8,128)}) fusion(f32[3,48,34,258]{2,1,0,3:T(8,128)} %bitcast.309), kind=kLoop, calls=%fused_computation.219 | loop fusion | bytes 589824 | tf_op jit(solution)/shard_map/slice | solution.py:125
  827.4 73.5 %all-reduce.14.cloned.1.call-done = bf16[3,4,48,256]{3,2,0,1:T(8,128)(2,1)} async-done(((bf16[3,4,48,256]{3,2,0,1:T(8,128)(2,1)}), bf16[3,4,48,256]{3,2,0,1:T(8,128)(2,1)}) %all-reduce.14.cloned.1.call-update) | async-done | bytes 294928 | tf_op jit(solution)/shard_map/psum | solution.py:59
  925.3 16.4 copy.2891
  948.4 16.5 slice.1002
  982.4 20.5 %slice_add_fusion.3 = f32[3,48,1,256]{2,1,0,3:T(8,128)} fusion(f32[3,48,1,256]{2,1,0,3:T(8,128)} %copy.2815, f32[3,48,34,258]{2,1,0,3:T(8,128)} %bitcast.315), kind=kLoop, calls=%fused_computation.14 | loop fusion | flops 36864 | bytes 442368 | tf_op jit(solution)/shard_map/add | solution.py:162
  1015.1 43.6 %scatter-add.94 = f32[3,48,32,256]{2,1,0,3:T(8,128)} dynamic-update-slice(f32[3,48,32,256]{2,1,0,3:T(8,128)} %slice.1002, f32[3,48,1,256]{2,1,0,3:T(8,128)} %slice_add_fusion.3, s32[]{:T(128)} %constant.616.clone.1, s32[]{:T(128)} %constant.616.clone.1, s32[]{:T(128)} %constant.616.clone.1, s32[]{:T(128)} %constant.616.clone.1) | dynamic-update-slice | bytes 294916 | tf_op jit(solution)/shard_map/scatter-add | solution.py:162
  1058.7 20.5 %slice_add_fusion.2 = f32[3,48,1,256]{2,1,0,3:T(8,128)} fusion(f32[3,48,1,256]{2,1,0,3:T(8,128)} %copy.2817, f32[3,48,32,256]{2,1,0,3:T(8,128)} %scatter-add.94), kind=kLoop, calls=%fused_computation.13 | loop fusion | flops 36864 | bytes 442368 | tf_op jit(solution)/shard_map/add | solution.py:163
  1079.2 73.5 %scatter-add.95 = f32[3,48,32,256]{2,1,0,3:T(8,128)} dynamic-update-slice(f32[3,48,32,256]{2,1,0,3:T(8,128)} %scatter-add.94, f32[3,48,1,256]{2,1,0,3:T(8,128)} %slice_add_fusion.2, s32[]{:T(128)} %constant.616.clone.1, s32[]{:T(128)} %constant.616.clone.1, s32[]{:T(128)} %constant.635.clone.1, s32[]{:T(128)} %constant.616.clone.1) | dynamic-update-slice | bytes 294916 | tf_op jit(solution)/shard_map/scatter-add | solution.py:163
  1207.4 44.8 %fusion.75 = f32[48,48,3,3]{0,1,3,2:T(8,128)} fusion(bf16[3,48,32,256]{1,0,3,2:T(4,128)(2,1)} %copy.2858, bf16[3,48,1,258]{1,0,3,2:T(4,128)(2,1)S(1)} %copy-done.15, bf16[3,48,32,1]{1,0,3,2:T(4,128)(2,1)S(1)} %copy-done.23, bf16[3,48,32,256]{1,0,3,2:T(4,128)(2,1)} %bitcast.319, bf16[3,48,32,1]{1,0,3,2:T(4,128)(2,1)S(1)} %copy-done.21, ...), kind=kOutput, calls=%fused_computation.227 | convolution fusion | flops 1031847552 | bytes 4968576 | tf_op jit(solution)/shard_map/conv_general_dilated | solution.py:172
  1252.2 15.0 copy.2857
  1287.3 14.3 reshape.1726
  1313.3 15.0 fusion.16
  1328.2 14.0 copy.2828
  1342.3 21.8 %convolution_select_fusion = f32[34,24,33,48]{3,1,2,0:T(8,128)} fusion(bf16[48,48,3,3]{1,0,3,2:T(8,128)(2,1)S(1)} %copy-done.48, bf16[48,34,3,8,35]{0,3,2,4,1:T(8,128)(2,1)} %copy.2828, pred[24,33]{0,1:T(8,128)(4,1)S(1)} %copy-done.52), kind=kOutput, calls=%fused_computation.36 | convolution fusion | flops 1096153344 | bytes 7954200 | tf_op jit(solution)/shard_map/conv_general_dilated | solution.py:34
  1377.7 15.7 reshape.1730
  1393.4 17.6 copy.2892
  1411.0 29.3 %fusion.66 = (f32[3,48,1,256]{2,1,0,3:T(8,128)}, f32[3,48,1,256]{2,1,0,3:T(8,128)}) fusion(f32[3,48,34,258]{2,1,0,3:T(8,128)} %bitcast.302), kind=kLoop, calls=%fused_computation.218 | loop fusion | bytes 589824 | tf_op jit(solution)/shard_map/slice | solution.py:125
  1475.0 44.8 %fusion.74 = f32[48,48,3,3]{0,1,3,2:T(8,128)} fusion(bf16[3,48,32,256]{1,0,3,2:T(4,128)(2,1)} %copy.2857, bf16[3,48,1,258]{1,0,3,2:T(4,128)(2,1)S(1)} %copy-done.11, bf16[3,48,32,1]{1,0,3,2:T(4,128)(2,1)S(1)} %copy-done.19, bf16[3,48,32,256]{1,0,3,2:T(4,128)(2,1)} %copy.2758, bf16[3,48,32,1]{1,0,3,2:T(4,128)(2,1)S(1)} %copy-done.17, ...), kind=kOutput, calls=%fused_computation.226 | convolution fusion | flops 1031847552 | bytes 4968576 | tf_op jit(solution)/shard_map/conv_general_dilated | solution.py:172
  1520.1 28.0 %all-reduce.16.cloned.1.call-done = bf16[3,4,48,256]{3,2,0,1:T(8,128)(2,1)} async-done(((bf16[3,4,48,256]{3,2,0,1:T(8,128)(2,1)}), bf16[3,4,48,256]{3,2,0,1:T(8,128)(2,1)}) %all-reduce.16.cloned.1.call-update) | async-done | bytes 294928 | tf_op jit(solution)/shard_map/psum | solution.py:59
  1567.8 39.3 %all-reduce.2 = (f32[48]{0:T(128)S(1)}, f32[48]{0:T(128)S(1)}) all-reduce(f32[48]{0:T(128)S(1)} %copy-done.46, f32[48]{0:T(128)S(1)} %copy-done.45), channel_id=1, replica_groups=mesh['face'=4,'tile'=8] {'face','tile'}, use_global_device_ids=true, to_apply=%region_6.7 | all-reduce | flops 96 | bytes 768 | tf_op jit(solution)/shard_map/psum | solution.py:219
  1608.2 16.6 slice.1030
  1624.8 54.6 %all-reduce.18.cloned.1.call-done = (f32[48,48,3,3]{0,1,3,2:T(8,128)}, f32[48,48,3,3]{0,1,3,2:T(8,128)}) async-done(((f32[48,48,3,3]{0,1,3,2:T(8,128)}, f32[48,48,3,3]{0,1,3,2:T(8,128)}), (f32[48,48,3,3]{0,1,3,2:T(8,128)}, f32[48,48,3,3]{0,1,3,2:T(8,128)})) %all-reduce.18.cloned.1.call-update) | async-done | bytes 165904 | tf_op jit(solution)/shard_map/psum | solution.py:219
  1683.0 60.5 %all-gather.11.cloned.1.call-done = bf16[3,4,48,1024]{2,1,0,3:T(4,128)(2,1)} async-done(((bf16[3,4,48,32]{2,1,0,3:T(4,128)(2,1)}), bf16[3,4,48,1024]{2,1,0,3:T(4,128)(2,1)}) %all-gather.11.cloned.1.call-update) | async-done | bytes 1179664 | tf_op jit(solution)/shard_map/all_gather | solution.py:71
  1760.5 20.5 %slice_add_fusion.1 = f32[3,48,1,256]{2,1,0,3:T(8,128)} fusion(f32[3,48,1,256]{2,1,0,3:T(8,128)} %copy.2852, f32[3,48,34,258]{2,1,0,3:T(8,128)} %bitcast.308), kind=kLoop, calls=%fused_computation.12 | loop fusion | flops 36864 | bytes 442368 | tf_op jit(solution)/shard_map/add | solution.py:162
  1793.2 43.6 %scatter-add.114 = f32[3,48,32,256]{2,1,0,3:T(8,128)} dynamic-update-slice(f32[3,48,32,256]{2,1,0,3:T(8,128)} %slice.1030, f32[3,48,1,256]{2,1,0,3:T(8,128)} %slice_add_fusion.1, s32[]{:T(128)} %constant.616.clone.1, s32[]{:T(128)} %constant.616.clone.1, s32[]{:T(128)} %constant.616.clone.1, s32[]{:T(128)} %constant.616.clone.1) | dynamic-update-slice | bytes 294916 | tf_op jit(solution)/shard_map/scatter-add | solution.py:162
  1836.8 20.5 %slice_add_fusion = f32[3,48,1,256]{2,1,0,3:T(8,128)} fusion(f32[3,48,1,256]{2,1,0,3:T(8,128)} %copy.2854, f32[3,48,32,256]{2,1,0,3:T(8,128)} %scatter-add.114), kind=kLoop, calls=%fused_computation.11 | loop fusion | flops 36864 | bytes 442368 | tf_op jit(solution)/shard_map/add | solution.py:163
  1857.3 73.6 %scatter-add.115 = f32[3,48,32,256]{2,1,0,3:T(8,128)} dynamic-update-slice(f32[3,48,32,256]{2,1,0,3:T(8,128)} %scatter-add.114, f32[3,48,1,256]{2,1,0,3:T(8,128)} %slice_add_fusion, s32[]{:T(128)} %constant.616.clone.1, s32[]{:T(128)} %constant.616.clone.1, s32[]{:T(128)} %constant.635.clone.1, s32[]{:T(128)} %constant.616.clone.1) | dynamic-update-slice | bytes 294916 | tf_op jit(solution)/shard_map/scatter-add | solution.py:163
  (349 shorter events, 505.5 us)
Async XLA Ops:
  7.2 552.0 %copy-start = (bf16[48,48,3,3]{1,0,3,2:T(8,128)(2,1)S(1)}, bf16[48,48,3,3]{1,0,3,2:T(8,128)(2,1)}, u32[]{:S(2)}) copy-start(bf16[48,48,3,3]{1,0,3,2:T(8,128)(2,1)} %param.60) | copy-start | bytes 124420
  7.2 88.4 %copy-start.4 = (bf16[3,48,32,256]{3,2,1,0:T(8,128)(2,1)S(1)}, bf16[3,48,32,256]{3,2,1,0:T(8,128)(2,1)}, u32[]{:S(2)}) copy-start(bf16[3,48,32,256]{3,2,1,0:T(8,128)(2,1)} %param.56) | copy-start | bytes 7077892
  7.2 86.5 %all-reduce.10.cloned.1.call-start = ((), (), s32[]{:S(2)}) async-start(), calls=%async_computation | async-start | bytes 589824 | tf_op jit(solution)/shard_map/psum | solution.py:59
  7.2 95.1 %copy-start.24 = (s32[12,4,3]{0,1,2:T(4,128)S(1)}, s32[12,4,3]{0,1,2:T(4,128)}, u32[]{:S(2)}) copy-start(s32[12,4,3]{0,1,2:T(4,128)} %param.62) | copy-start | bytes 1732
  7.3 96.2 %copy-start.44 = (s32[12,4]{0,1:T(4,128)S(1)}, s32[12,4]{0,1:T(4,128)}, u32[]{:S(2)}) copy-start(s32[12,4]{0,1:T(4,128)} %param.63) | copy-start | bytes 580
  19.2 136.6 %all-gather.5.cloned.1.call-start = ((), (), s32[]{:S(2)}) async-start(), calls=%async_computation.1 | async-start | bytes 3244032 | tf_op jit(solution)/shard_map/all_gather | solution.py:71
  95.5 288.3 %all-reduce.12.cloned.1.call-start = ((), (), s32[]{:S(2)}) async-start(), calls=%async_computation.2 | async-start | bytes 589824 | tf_op jit(solution)/shard_map/psum | solution.py:59
  103.4 345.7 %copy-start.25 = (pred[12]{0:T(512)(128)(4,1)}, pred[12]{0:T(512)(128)(4,1)S(1)}, u32[]{:S(2)}) copy-start(pred[12]{0:T(512)(128)(4,1)S(1)} %eq.133) | copy-start | bytes 40
  103.9 341.5 %copy-start.5 = (s32[12]{0:T(128)}, s32[12]{0:T(128)S(1)}, u32[]{:S(2)}) copy-start(s32[12]{0:T(128)S(1)} %fusion.63) | copy-start | bytes 148
  161.7 35.6 %copy-start.16 = (bf16[3,48,32,1]{1,0,3,2:T(4,128)(2,1)}, bf16[3,48,32,1]{1,0,3,2:T(4,128)(2,1)S(1)}, u32[]{:S(2)}) copy-start(bf16[3,48,32,1]{1,0,3,2:T(4,128)(2,1)S(1)} %copy.2757) | copy-start | bytes 27652
  161.8 35.5 %copy-start.18 = (bf16[3,48,32,1]{1,0,3,2:T(4,128)(2,1)}, bf16[3,48,32,1]{1,0,3,2:T(4,128)(2,1)S(1)}, u32[]{:S(2)}) copy-start(bf16[3,48,32,1]{1,0,3,2:T(4,128)(2,1)S(1)} %copy.2759) | copy-start | bytes 27652
  163.5 15.4 collective-permute-start
  167.1 12.0 collective-permute-start.1
  179.2 24.7 %copy-start.8 = (bf16[3,48,1,258]{1,0,3,2:T(4,128)(2,1)}, bf16[3,48,1,258]{1,0,3,2:T(4,128)(2,1)S(1)}, u32[]{:S(2)}) copy-start(bf16[3,48,1,258]{1,0,3,2:T(4,128)(2,1)S(1)} %maximum_select_fusion) | copy-start | bytes 222916
  179.5 24.5 %copy-start.10 = (bf16[3,48,1,258]{1,0,3,2:T(4,128)(2,1)}, bf16[3,48,1,258]{1,0,3,2:T(4,128)(2,1)S(1)}, u32[]{:S(2)}) copy-start(bf16[3,48,1,258]{1,0,3,2:T(4,128)(2,1)S(1)} %maximum_select_fusion.1) | copy-start | bytes 222916
  311.7 133.7 %all-gather.7.cloned.1.call-start = ((), (), s32[]{:S(2)}) async-start(), calls=%async_computation.3 | async-start | bytes 3244032 | tf_op jit(solution)/shard_map/all_gather | solution.py:71
  385.6 515.3 %all-reduce.14.cloned.1.call-start = ((), (), s32[]{:S(2)}) async-start(), calls=%async_computation.4 | async-start | bytes 589824 | tf_op jit(solution)/shard_map/psum | solution.py:59
  451.3 36.4 %copy-start.20 = (bf16[3,48,32,1]{1,0,3,2:T(4,128)(2,1)}, bf16[3,48,32,1]{1,0,3,2:T(4,128)(2,1)S(1)}, u32[]{:S(2)}) copy-start(bf16[3,48,32,1]{1,0,3,2:T(4,128)(2,1)S(1)} %copy.2778) | copy-start | bytes 27652
  451.4 36.3 %copy-start.22 = (bf16[3,48,32,1]{1,0,3,2:T(4,128)(2,1)}, bf16[3,48,32,1]{1,0,3,2:T(4,128)(2,1)S(1)}, u32[]{:S(2)}) copy-start(bf16[3,48,32,1]{1,0,3,2:T(4,128)(2,1)S(1)} %copy.2779) | copy-start | bytes 27652
  452.9 15.1 collective-permute-start.2
  456.3 12.0 collective-permute-start.3
  468.3 26.1 %copy-start.12 = (bf16[3,48,1,258]{1,0,3,2:T(4,128)(2,1)}, bf16[3,48,1,258]{1,0,3,2:T(4,128)(2,1)S(1)}, u32[]{:S(2)}) copy-start(bf16[3,48,1,258]{1,0,3,2:T(4,128)(2,1)S(1)} %maximum_select_fusion.2) | copy-start | bytes 222916
  468.5 25.8 %copy-start.14 = (bf16[3,48,1,258]{1,0,3,2:T(4,128)(2,1)}, bf16[3,48,1,258]{1,0,3,2:T(4,128)(2,1)S(1)}, u32[]{:S(2)}) copy-start(bf16[3,48,1,258]{1,0,3,2:T(4,128)(2,1)S(1)} %maximum_select_fusion.3) | copy-start | bytes 222916
  621.4 13.5 collective-permute-start.4
  625.8 9.1 collective-permute-start.5
  627.4 192.8 %copy-start.38 = (pred[3]{0:T(512)(128)(4,1)}, pred[3]{0:T(512)(128)(4,1)S(1)}, u32[]{:S(2)}) copy-start(pred[3]{0:T(512)(128)(4,1)S(1)} %get-tuple-element.458) | copy-start | bytes 13
  627.4 192.8 %copy-start.40 = (pred[3]{0:T(512)(128)(4,1)}, pred[3]{0:T(512)(128)(4,1)S(1)}, u32[]{:S(2)}) copy-start(pred[3]{0:T(512)(128)(4,1)S(1)} %get-tuple-element.462) | copy-start | bytes 13
  627.4 192.8 %copy-start.42 = (pred[3]{0:T(512)(128)(4,1)}, pred[3]{0:T(512)(128)(4,1)S(1)}, u32[]{:S(2)}) copy-start(pred[3]{0:T(512)(128)(4,1)S(1)} %get-tuple-element.463) | copy-start | bytes 13
  627.5 194.5 %copy-start.30 = (pred[3]{0:T(512)(128)(4,1)}, pred[3]{0:T(512)(128)(4,1)S(1)}, u32[]{:S(2)}) copy-start(pred[3]{0:T(512)(128)(4,1)S(1)} %get-tuple-element.456) | copy-start | bytes 13
  627.5 194.5 %copy-start.32 = (pred[3]{0:T(512)(128)(4,1)}, pred[3]{0:T(512)(128)(4,1)S(1)}, u32[]{:S(2)}) copy-start(pred[3]{0:T(512)(128)(4,1)S(1)} %get-tuple-element.457) | copy-start | bytes 13
  627.5 194.5 %copy-start.34 = (pred[3]{0:T(512)(128)(4,1)}, pred[3]{0:T(512)(128)(4,1)S(1)}, u32[]{:S(2)}) copy-start(pred[3]{0:T(512)(128)(4,1)S(1)} %get-tuple-element.460) | copy-start | bytes 13
  627.5 194.5 %copy-start.36 = (pred[3]{0:T(512)(128)(4,1)}, pred[3]{0:T(512)(128)(4,1)S(1)}, u32[]{:S(2)}) copy-start(pred[3]{0:T(512)(128)(4,1)S(1)} %get-tuple-element.461) | copy-start | bytes 13
  627.5 196.7 %copy-start.28 = (pred[3]{0:T(512)(128)(4,1)}, pred[3]{0:T(512)(128)(4,1)S(1)}, u32[]{:S(2)}) copy-start(pred[3]{0:T(512)(128)(4,1)S(1)} %get-tuple-element.459) | copy-start | bytes 13
  827.4 137.6 %all-gather.9.cloned.1.call-start = ((), (), s32[]{:S(2)}) async-start(), calls=%async_computation.5 | async-start | bytes 3244032 | tf_op jit(solution)/shard_map/all_gather | solution.py:71
  902.8 645.3 %all-reduce.16.cloned.1.call-start = ((), (), s32[]{:S(2)}) async-start(), calls=%async_computation.6 | async-start | bytes 589824 | tf_op jit(solution)/shard_map/psum | solution.py:59
  1179.0 28.3 %copy-start.13 = (bf16[3,48,1,258]{1,0,3,2:T(4,128)(2,1)S(1)}, bf16[3,48,1,258]{1,0,3,2:T(4,128)(2,1)}, u32[]{:S(2)}) copy-start(bf16[3,48,1,258]{1,0,3,2:T(4,128)(2,1)} %copy-done.12) | copy-start | bytes 222916
  1179.0 28.3 %copy-start.15 = (bf16[3,48,1,258]{1,0,3,2:T(4,128)(2,1)S(1)}, bf16[3,48,1,258]{1,0,3,2:T(4,128)(2,1)}, u32[]{:S(2)}) copy-start(bf16[3,48,1,258]{1,0,3,2:T(4,128)(2,1)} %copy-done.14) | copy-start | bytes 222916
  1179.0 28.3 %copy-start.21 = (bf16[3,48,32,1]{1,0,3,2:T(4,128)(2,1)S(1)}, bf16[3,48,32,1]{1,0,3,2:T(4,128)(2,1)}, u32[]{:S(2)}) copy-start(bf16[3,48,32,1]{1,0,3,2:T(4,128)(2,1)} %copy-done.20) | copy-start | bytes 27652
  1179.1 28.3 %copy-start.23 = (bf16[3,48,32,1]{1,0,3,2:T(4,128)(2,1)S(1)}, bf16[3,48,32,1]{1,0,3,2:T(4,128)(2,1)}, u32[]{:S(2)}) copy-start(bf16[3,48,32,1]{1,0,3,2:T(4,128)(2,1)} %copy-done.22) | copy-start | bytes 27652
  1191.2 90.2 %collective-permute-start.6 = (bf16[3,48,1,258]{3,1,2,0:T(8,128)(2,1)}, bf16[3,48,1,258]{3,1,2,0:T(8,128)(2,1)}, u32[]{:S(2)}, u32[]{:S(2)}) collective-permute-start(bf16[3,48,1,258]{3,1,2,0:T(8,128)(2,1)} %copy.2824), channel_id=1, source_target_pairs={{0,1},{1,2},{2,3},{3,4},{4,5},{5,6},{6,7},{8,9},{9,10},{10,11},{11... | collective-permute-start | bytes 222920 | tf_op jit(solution)/shard_map/ppermute | solution.py:19
  1206.1 75.3 %collective-permute-start.7 = (bf16[3,48,1,258]{3,1,2,0:T(8,128)(2,1)}, bf16[3,48,1,258]{3,1,2,0:T(8,128)(2,1)}, u32[]{:S(2)}, u32[]{:S(2)}) collective-permute-start(bf16[3,48,1,258]{3,1,2,0:T(8,128)(2,1)} %copy.2825), channel_id=1, source_target_pairs={{1,0},{2,1},{3,2},{4,3},{5,4},{6,5},{7,6},{9,8},{10,9},{11,10},{12... | collective-permute-start | bytes 222920 | tf_op jit(solution)/shard_map/ppermute | solution.py:22
  1411.0 29.3 %copy-start.39 = (pred[3]{0:T(512)(128)(4,1)S(1)}, pred[3]{0:T(512)(128)(4,1)}, u32[]{:S(2)}) copy-start(pred[3]{0:T(512)(128)(4,1)} %copy-done.38) | copy-start | bytes 13
  1411.0 29.3 %copy-start.41 = (pred[3]{0:T(512)(128)(4,1)S(1)}, pred[3]{0:T(512)(128)(4,1)}, u32[]{:S(2)}) copy-start(pred[3]{0:T(512)(128)(4,1)} %copy-done.40) | copy-start | bytes 13
  1411.0 29.3 %copy-start.43 = (pred[3]{0:T(512)(128)(4,1)S(1)}, pred[3]{0:T(512)(128)(4,1)}, u32[]{:S(2)}) copy-start(pred[3]{0:T(512)(128)(4,1)} %copy-done.42) | copy-start | bytes 13
  1474.9 204.5 %all-reduce.18.cloned.1.call-start = ((), (), s32[]{:S(2)}) async-start(), calls=%async_computation.8 | async-start | bytes 884736 | tf_op jit(solution)/shard_map/psum | solution.py:219
  1519.8 223.6 %all-gather.11.cloned.1.call-start = ((), (), s32[]{:S(2)}) async-start(), calls=%async_computation.7 | async-start | bytes 3244032 | tf_op jit(solution)/shard_map/all_gather | solution.py:71
  1608.2 135.2 %copy-start.7 = (s32[12]{0:T(128)S(1)}, s32[12]{0:T(128)}, u32[]{:S(2)}) copy-start(s32[12]{0:T(128)} %copy-done.5) | copy-start | bytes 148
  1608.2 139.0 %copy-start.27 = (pred[12]{0:T(512)(128)(4,1)S(1)}, pred[12]{0:T(512)(128)(4,1)}, u32[]{:S(2)}) copy-start(pred[12]{0:T(512)(128)(4,1)} %copy-done.25) | copy-start | bytes 40
  (23 other events, 361.3 us)
Sparse Core Ops, SparseCore 0:
  19.3 74.3 all-reduce.9
  97.6 58.1 all-gather.4
  311.8 71.9 all-reduce.11
  387.2 58.1 all-gather.6
  827.5 73.4 all-reduce.13
  904.7 58.1 all-gather.8
  1475.0 72.9 all-reduce.15
  1554.0 125.3 all-reduce.17
  1683.3 60.0 all-gather.10
where the time goes:
time: 1990 us; the launch traced here: 1960 us
  local copies, waits for them, and re-layouts  973 us (49%)
  waiting for transfers between devices  499 us (25%)
  other arithmetic  236 us (12%)
  matrix products  179 us (9%)
  blocking collectives  39.3 us (2%)
  starting transfers between devices  21.1 us (1%)
    psum x4, waiting for transfers between devices, place_lines(): own_lines = lax.psum(placed.astype(jnp.bfloat16), 'tile')  248 us
    conv_general_dilated x16, local copies, waits for them, and re-layouts, convolve(): lax.conv_general_dilated(padded, weight, (1, 1), 'VALID', dimension_numbe...  238 us
    all_gather x4, waiting for transfers between devices, partner_pieces(): gathered = lax.all_gather(front, ('face', 'tile'), axis=3, tiled=True)  172 us
    scatter-add x2, local copies, waits for them, and re-layouts, unfold_strip(): interior.at[:, :, -1, :]  147 us
    unnamed x128, local copies, waits for them, and re-layouts  125 us
    conv_general_dilated x4, matrix products, convolve(): lax.conv_general_dilated(padded, weight, (1, 1), 'VALID', dimension_numbe...  89.7 us
    conv_general_dilated x2, matrix products, weight_grad(): lax.conv_general_dilated(padded, cotangent, (1, 1), 'VALID', dimension_nu...  89.7 us
    scatter-add x2, local copies, waits for them, and re-layouts, unfold_strip(): interior.at[:, :, 0, :]  87.2 us
  transfers between devices with their start and end apart: 17, of which 11 were waited for; matrix products, arithmetic and copies ran while one was open for 13% of the time, Pallas kernels for 0%

commit v1 on v0

--- a/solution.py
+++ b/solution.py
@@ -5,6 +5,18 @@
 
 INV_ROOT_TWO = 0.7071067811865476
 INV_ROOT_TWO_PI = 0.3989422804014327
+
+
+def collect(shard, axis, dim):
+    ways, here, hop = (lax.axis_size(axis), lax.axis_index(axis), shard.shape[dim])
+    line, have = (shard, 1)
+    while have < ways:
+        line = jnp.concatenate(
+            [line, lax.ppermute(line, axis, [(d, (d - have) % ways) for d in range(ways)])],
+            axis=dim,
+        )
+        have = 2 * have
+    return jnp.roll(line, here * hop, axis=dim)
 
 
 def shortened(x):
@@ -68,7 +80,7 @@
     partner_face = my_links[:, :, 0].reshape(-1)
     partner_edge = my_links[:, :, 1].reshape(-1)
     flip_mask = (my_links[:, :, 2] == 1).reshape(-1)
-    gathered = lax.all_gather(front, ("face", "tile"), axis=3, tiled=True)
+    gathered = collect(front, ("face", "tile"), 3)
 
     def fetch_line(face_id, edge_id):
         start = (face_id % faces_dev, edge_id, 0, face_id // faces_dev * side_len)

time: 1990 us -> 2030 us (1.020)
  waiting for transfers between devices: 499 us -> 467 us
  local copies, waits for them, and re-layouts: 973 us -> 999 us
  starting transfers between devices: 21.1 us -> 44.4 us
  other arithmetic: 236 us -> 259 us
    all_gather x4 -> x0, waiting for transfers between devices: 172 us -> none  [partner_pieces(): gathered = lax.all_gather(front, ('face', 'tile'), axis=3, tiled=True)]
    ppermute x0 -> x20, waiting for transfers between devices: none -> 88.3 us  [collect(): lax.ppermute(line, axis, [(d, (d - have) % ways) for d in range(ways)])]
    psum x4, waiting for transfers between devices: 248 us -> 290 us  [place_lines(): own_lines = lax.psum(placed.astype(jnp.bfloat16), 'tile')]
    unnamed x128 -> x158, local copies, waits for them, and re-layouts: 125 us -> 144 us
  transfers between devices with their start and end apart: 17 -> 33, of which waited for: 11 -> 22; matrix products, arithmetic and copies ran while one was open for 13% -> 12% of each run, Pallas kernels for 0% -> 0%
where the time goes in v1:
time: 2030 us; the launch traced here: 2010 us
  local copies, waits for them, and re-layouts  999 us (49%)
  waiting for transfers between devices  467 us (23%)
  other arithmetic  259 us (13%)
  matrix products  180 us (9%)
  starting transfers between devices  44.4 us (2%)
  blocking collectives  39.9 us (2%)
    psum x4, waiting for transfers between devices, place_lines(): own_lines = lax.psum(placed.astype(jnp.bfloat16), 'tile')  290 us
    conv_general_dilated x16, local copies, waits for them, and re-layouts, convolve(): lax.conv_general_dilated(padded, weight, (1, 1), 'VALID', dimension_numbe...  238 us
    scatter-add x2, local copies, waits for them, and re-layouts, unfold_strip(): interior.at[:, :, -1, :]  147 us
    unnamed x158, local copies, waits for them, and re-layouts  144 us
    conv_general_dilated x4, matrix products, convolve(): lax.conv_general_dilated(padded, weight, (1, 1), 'VALID', dimension_numbe...  90.3 us
    conv_general_dilated x2, matrix products, weight_grad(): lax.conv_general_dilated(padded, cotangent, (1, 1), 'VALID', dimension_nu...  90.1 us
    ppermute x20, waiting for transfers between devices, collect(): lax.ppermute(line, axis, [(d, (d - have) % ways) for d in range(ways)])  88.3 us
    scatter-add x2, local copies, waits for them, and re-layouts, unfold_strip(): interior.at[:, :, 0, :]  87.2 us
  transfers between devices with their start and end apart: 33, of which 22 were waited for; matrix products, arithmetic and copies ran while one was open for 12% of the time, Pallas kernels for 0%

profile of v1, /device:TPU:0, one launch (start us, length us, event | category | flops | bytes accessed | tf_op | source)
XLA Modules:
  0.0 2005.1 jit_solution(7548753112284373707)
XLA Ops:
  19.2 74.5 %all-reduce.10.cloned.1.call-done = bf16[3,4,48,256]{3,2,1,0:T(8,128)(2,1)} async-done(((bf16[3,4,48,256]{3,2,1,0:T(8,128)(2,1)}), bf16[3,4,48,256]{3,2,1,0:T(8,128)(2,1)}) %all-reduce.10.cloned.1.call-update) | async-done | bytes 294928 | tf_op jit(solution)/shard_map/psum | solution.py:71
  175.2 19.1 fusion.91
  201.0 24.2 %copy.2911 = bf16[48,34,3,8,33]{4,3,0,2,1:T(8,128)(2,1)} copy(bf16[48,34,3,8,33]{0,2,4,3,1:T(4,128)(2,1)} %bitcast.334) | data formatting | bytes 5170176 | tf_op jit(solution)/shard_map/conv_general_dilated | solution.py:46
  236.9 14.9 fusion.13
  251.8 14.0 copy.2804
  265.9 23.6 %fusion.8 = (f32[32,24,33,48]{3,1,2,0:T(8,128)}, bf16[32,24,33,48]{3,1,2,0:T(8,128)(2,1)S(1)}) fusion(f32[48]{0:T(128)S(1)} %copy-done.62, pred[24,33]{0,1:T(8,128)(4,1)S(1)} %copy-done.66, bf16[48,48,3,3]{1,0,3,2:T(8,128)(2,1)S(1)} %copy-done.60, bf16[48,34,3,8,35]{0,3,2,4,1:T(8,128)(2,1)} %copy.2804), kind=kOutput, calls=%fused_computation.21 | convolution fusion | flops 1065664512 | bytes 10083288 | tf_op jit(solution)/shard_map/conv_general_dilated | solution.py:46
  309.1 71.0 %all-reduce.12.cloned.1.call-done = bf16[3,4,48,256]{3,2,1,0:T(8,128)(2,1)} async-done(((bf16[3,4,48,256]{3,2,1,0:T(8,128)(2,1)}), bf16[3,4,48,256]{3,2,1,0:T(8,128)(2,1)}) %all-reduce.12.cloned.1.call-update) | async-done | bytes 294928 | tf_op jit(solution)/shard_map/psum | solution.py:71
  408.3 13.7 collective-permute-done.11
  457.9 19.3 fusion.88
  483.8 24.2 %copy.2920 = bf16[48,34,3,8,33]{4,3,0,2,1:T(8,128)(2,1)} copy(bf16[48,34,3,8,33]{0,2,4,3,1:T(4,128)(2,1)} %bitcast.335) | data formatting | bytes 5170176 | tf_op jit(solution)/shard_map/conv_general_dilated | solution.py:46
  519.8 14.9 fusion.14
  534.7 14.0 copy.2826
  548.7 22.5 %fusion.12 = (f32[32,24,33,48]{3,1,2,0:T(8,128)}, bf16[32,24,33,48]{3,1,2,0:T(8,128)(2,1)}) fusion(f32[48]{0:T(128)S(1)} %copy-done.63, pred[24,33]{0,1:T(8,128)(4,1)S(1)} %copy-done.66, bf16[48,48,3,3]{1,0,3,2:T(8,128)(2,1)S(1)} %copy-done, bf16[48,34,3,8,35]{0,3,2,4,1:T(8,128)(2,1)} %copy.2826), kind=kOutput, calls=%fused_computation.25 | convolution fusion | flops 1065664512 | bytes 10083288 | tf_op jit(solution)/shard_map/conv_general_dilated | solution.py:46
  628.9 14.1 reshape.1719
  654.7 14.9 fusion.15
  669.6 14.0 copy.2834
  683.6 22.2 %convolution_select_fusion.1 = f32[34,24,33,48]{3,1,2,0:T(8,128)} fusion(bf16[48,48,3,3]{1,0,3,2:T(8,128)(2,1)S(1)} %copy-done, bf16[48,34,3,8,35]{0,3,2,4,1:T(8,128)(2,1)} %copy.2834, pred[24,33]{0,1:T(8,128)(4,1)S(1)} %copy-done.64), kind=kOutput, calls=%fused_computation.37 | convolution fusion | flops 1096153344 | bytes 7954200 | tf_op jit(solution)/shard_map/conv_general_dilated | solution.py:46
  705.8 13.6 copy.2835
  719.4 15.7 reshape.1723
  735.1 17.6 copy.2942
  752.7 29.0 %fusion.71 = (f32[3,48,1,256]{2,1,0,3:T(8,128)}, f32[3,48,1,256]{2,1,0,3:T(8,128)}) fusion(f32[3,48,34,258]{2,1,0,3:T(8,128)} %bitcast.319), kind=kLoop, calls=%fused_computation.239 | loop fusion | bytes 589824 | tf_op jit(solution)/shard_map/slice | solution.py:137
  816.3 71.8 %all-reduce.14.cloned.1.call-done = bf16[3,4,48,256]{3,2,1,0:T(8,128)(2,1)} async-done(((bf16[3,4,48,256]{3,2,1,0:T(8,128)(2,1)}), bf16[3,4,48,256]{3,2,1,0:T(8,128)(2,1)}) %all-reduce.14.cloned.1.call-update) | async-done | bytes 294928 | tf_op jit(solution)/shard_map/psum | solution.py:71
  938.5 16.2 copy.2944
  954.7 16.4 slice.1002
  998.7 20.5 %slice_add_fusion.3 = f32[3,48,1,256]{2,1,0,3:T(8,128)} fusion(f32[3,48,1,256]{2,1,0,3:T(8,128)} %copy.2860, f32[3,48,34,258]{2,1,0,3:T(8,128)} %bitcast.325), kind=kLoop, calls=%fused_computation.14 | loop fusion | flops 36864 | bytes 442368 | tf_op jit(solution)/shard_map/add | solution.py:174
  1031.3 43.6 %scatter-add.94 = f32[3,48,32,256]{2,1,0,3:T(8,128)} dynamic-update-slice(f32[3,48,32,256]{2,1,0,3:T(8,128)} %slice.1002, f32[3,48,1,256]{2,1,0,3:T(8,128)} %slice_add_fusion.3, s32[]{:T(128)} %constant.634.clone.1, s32[]{:T(128)} %constant.634.clone.1, s32[]{:T(128)} %constant.634.clone.1, s32[]{:T(128)} %constant.634.clone.1) | dynamic-update-slice | bytes 294916 | tf_op jit(solution)/shard_map/scatter-add | solution.py:174
  1074.9 20.5 %slice_add_fusion.2 = f32[3,48,1,256]{2,1,0,3:T(8,128)} fusion(f32[3,48,1,256]{2,1,0,3:T(8,128)} %copy.2861, f32[3,48,32,256]{2,1,0,3:T(8,128)} %scatter-add.94), kind=kLoop, calls=%fused_computation.13 | loop fusion | flops 36864 | bytes 442368 | tf_op jit(solution)/shard_map/add | solution.py:175
  1095.4 73.6 %scatter-add.95 = f32[3,48,32,256]{2,1,0,3:T(8,128)} dynamic-update-slice(f32[3,48,32,256]{2,1,0,3:T(8,128)} %scatter-add.94, f32[3,48,1,256]{2,1,0,3:T(8,128)} %slice_add_fusion.2, s32[]{:T(128)} %constant.634.clone.1, s32[]{:T(128)} %constant.634.clone.1, s32[]{:T(128)} %constant.654.clone.1, s32[]{:T(128)} %constant.634.clone.1) | dynamic-update-slice | bytes 294916 | tf_op jit(solution)/shard_map/scatter-add | solution.py:175
  1243.5 14.1 reshape.1726
  1269.3 14.9 fusion.16
  1284.3 14.0 copy.2872
  1298.3 22.0 %convolution_select_fusion = f32[34,24,33,48]{3,1,2,0:T(8,128)} fusion(bf16[48,48,3,3]{1,0,3,2:T(8,128)(2,1)S(1)} %copy-done.61, bf16[48,34,3,8,35]{0,3,2,4,1:T(8,128)(2,1)} %copy.2872, pred[24,33]{0,1:T(8,128)(4,1)S(1)} %copy-done.65), kind=kOutput, calls=%fused_computation.36 | convolution fusion | flops 1096153344 | bytes 7954200 | tf_op jit(solution)/shard_map/conv_general_dilated | solution.py:46
  1320.3 13.6 copy.2873
  1333.9 15.7 reshape.1730
  1349.6 17.6 copy.2945
  1367.2 29.2 %fusion.70 = (f32[3,48,1,256]{2,1,0,3:T(8,128)}, f32[3,48,1,256]{2,1,0,3:T(8,128)}) fusion(f32[3,48,34,258]{2,1,0,3:T(8,128)} %bitcast.312), kind=kLoop, calls=%fused_computation.238 | loop fusion | bytes 589824 | tf_op jit(solution)/shard_map/slice | solution.py:137
  1412.5 13.4 copy.2875
  1435.1 72.9 %all-reduce.16.cloned.1.call-done = bf16[3,4,48,256]{3,2,1,0:T(8,128)(2,1)} async-done(((bf16[3,4,48,256]{3,2,1,0:T(8,128)(2,1)}), bf16[3,4,48,256]{3,2,1,0:T(8,128)(2,1)}) %all-reduce.16.cloned.1.call-update) | async-done | bytes 294928 | tf_op jit(solution)/shard_map/psum | solution.py:71
  1518.8 45.2 %fusion.79 = f32[48,48,3,3]{0,1,3,2:T(8,128)} fusion(bf16[3,48,32,256]{1,0,3,2:T(4,128)(2,1)} %copy.2902, bf16[3,48,1,258]{1,0,3,2:T(4,128)(2,1)S(1)} %copy-done.26, bf16[3,48,32,1]{1,0,3,2:T(4,128)(2,1)S(1)} %copy-done.34, bf16[3,48,32,256]{1,0,3,2:T(4,128)(2,1)} %bitcast.329, bf16[3,48,32,1]{1,0,3,2:T(4,128)(2,1)S(1)} %copy-done.32, ...), kind=kOutput, calls=%fused_computation.247 | convolution fusion | flops 1031847552 | bytes 4968576 | tf_op jit(solution)/shard_map/conv_general_dilated | solution.py:184
  1580.3 15.1 copy.2901
  1600.3 44.9 %fusion.78 = f32[48,48,3,3]{0,1,3,2:T(8,128)} fusion(bf16[3,48,32,256]{1,0,3,2:T(4,128)(2,1)} %copy.2901, bf16[3,48,1,258]{1,0,3,2:T(4,128)(2,1)S(1)} %copy-done.22, bf16[3,48,32,1]{1,0,3,2:T(4,128)(2,1)S(1)} %copy-done.30, bf16[3,48,32,256]{1,0,3,2:T(4,128)(2,1)} %copy.2800, bf16[3,48,32,1]{1,0,3,2:T(4,128)(2,1)S(1)} %copy-done.28, ...), kind=kOutput, calls=%fused_computation.246 | convolution fusion | flops 1031847552 | bytes 4968576 | tf_op jit(solution)/shard_map/conv_general_dilated | solution.py:184
  1645.2 39.9 %all-reduce.2 = (f32[48]{0:T(128)S(1)}, f32[48]{0:T(128)S(1)}) all-reduce(f32[48]{0:T(128)S(1)} %copy-done.59, f32[48]{0:T(128)S(1)} %copy-done.58), channel_id=1, replica_groups=mesh['face'=4,'tile'=8] {'face','tile'}, use_global_device_ids=true, to_apply=%region_6.8 | all-reduce | flops 96 | bytes 768 | tf_op jit(solution)/shard_map/psum | solution.py:231
  1689.8 16.5 slice.1030
  1706.3 64.0 %all-reduce.18.cloned.1.call-done = (f32[48,48,3,3]{0,1,3,2:T(8,128)}, f32[48,48,3,3]{0,1,3,2:T(8,128)}) async-done(((f32[48,48,3,3]{0,1,3,2:T(8,128)}, f32[48,48,3,3]{0,1,3,2:T(8,128)}), (f32[48,48,3,3]{0,1,3,2:T(8,128)}, f32[48,48,3,3]{0,1,3,2:T(8,128)})) %all-reduce.18.cloned.1.call-update) | async-done | bytes 165904 | tf_op jit(solution)/shard_map/psum | solution.py:231
  1802.5 20.5 %slice_add_fusion.1 = f32[3,48,1,256]{2,1,0,3:T(8,128)} fusion(f32[3,48,1,256]{2,1,0,3:T(8,128)} %copy.2897, f32[3,48,34,258]{2,1,0,3:T(8,128)} %bitcast.318), kind=kLoop, calls=%fused_computation.12 | loop fusion | flops 36864 | bytes 442368 | tf_op jit(solution)/shard_map/add | solution.py:174
  1835.0 43.6 %scatter-add.114 = f32[3,48,32,256]{2,1,0,3:T(8,128)} dynamic-update-slice(f32[3,48,32,256]{2,1,0,3:T(8,128)} %slice.1030, f32[3,48,1,256]{2,1,0,3:T(8,128)} %slice_add_fusion.1, s32[]{:T(128)} %constant.634.clone.1, s32[]{:T(128)} %constant.634.clone.1, s32[]{:T(128)} %constant.634.clone.1, s32[]{:T(128)} %constant.634.clone.1) | dynamic-update-slice | bytes 294916 | tf_op jit(solution)/shard_map/scatter-add | solution.py:174
  1878.6 20.5 %slice_add_fusion = f32[3,48,1,256]{2,1,0,3:T(8,128)} fusion(f32[3,48,1,256]{2,1,0,3:T(8,128)} %copy.2898, f32[3,48,32,256]{2,1,0,3:T(8,128)} %scatter-add.114), kind=kLoop, calls=%fused_computation.11 | loop fusion | flops 36864 | bytes 442368 | tf_op jit(solution)/shard_map/add | solution.py:175
  1899.0 73.5 %scatter-add.115 = f32[3,48,32,256]{2,1,0,3:T(8,128)} dynamic-update-slice(f32[3,48,32,256]{2,1,0,3:T(8,128)} %scatter-add.114, f32[3,48,1,256]{2,1,0,3:T(8,128)} %slice_add_fusion, s32[]{:T(128)} %constant.634.clone.1, s32[]{:T(128)} %constant.634.clone.1, s32[]{:T(128)} %constant.654.clone.1, s32[]{:T(128)} %constant.634.clone.1) | dynamic-update-slice | bytes 294916 | tf_op jit(solution)/shard_map/scatter-add | solution.py:175
  (427 shorter events, 624.8 us)
Async XLA Ops:
  7.2 541.5 %copy-start = (bf16[48,48,3,3]{1,0,3,2:T(8,128)(2,1)S(1)}, bf16[48,48,3,3]{1,0,3,2:T(8,128)(2,1)}, u32[]{:S(2)}) copy-start(bf16[48,48,3,3]{1,0,3,2:T(8,128)(2,1)} %param.62) | copy-start | bytes 124420
  7.2 116.4 %copy-start.5 = (bf16[3,48,32,256]{3,2,1,0:T(8,128)(2,1)S(1)}, bf16[3,48,32,256]{3,2,1,0:T(8,128)(2,1)}, u32[]{:S(2)}) copy-start(bf16[3,48,32,256]{3,2,1,0:T(8,128)(2,1)} %param.58) | copy-start | bytes 7077892
  7.2 116.3 %copy-start.35 = (s32[12,4,3]{0,1,2:T(4,128)S(1)}, s32[12,4,3]{0,1,2:T(4,128)}, u32[]{:S(2)}) copy-start(s32[12,4,3]{0,1,2:T(4,128)} %param.64) | copy-start | bytes 1732
  7.2 86.5 %all-reduce.10.cloned.1.call-start = ((), (), s32[]{:S(2)}) async-start(), calls=%async_computation | async-start | bytes 589824 | tf_op jit(solution)/shard_map/psum | solution.py:71
  11.0 120.9 %copy-start.57 = (s32[12,4]{0,1:T(4,128)S(1)}, s32[12,4]{0,1:T(4,128)}, u32[]{:S(2)}) copy-start(s32[12,4]{0,1:T(4,128)} %param.65) | copy-start | bytes 580
  19.2 360.9 %all-reduce.12.cloned.1.call-start = ((), (), s32[]{:S(2)}) async-start(), calls=%async_computation.1 | async-start | bytes 589824 | tf_op jit(solution)/shard_map/psum | solution.py:71
  94.7 5.2 collective-permute-start
  100.0 5.9 collective-permute-start.1
  106.1 9.1 collective-permute-start.2
  116.1 4.7 collective-permute-start.3
  121.9 15.8 collective-permute-start.4
  133.4 295.8 %copy-start.14 = (s32[12]{0:T(128)}, s32[12]{0:T(128)S(1)}, u32[]{:S(2)}) copy-start(s32[12]{0:T(128)S(1)} %fusion.67) | copy-start | bytes 148
  156.6 18.0 collective-permute-start.5
  163.1 11.8 collective-permute-start.6
  294.5 113.7 %copy-start.39 = (s32[3,4]{0,1:T(4,128)S(1)}, s32[3,4]{0,1:T(4,128)}, u32[]{:S(2)}) copy-start(s32[3,4]{0,1:T(4,128)} %get-tuple-element.478) | copy-start | bytes 148
  307.0 126.9 %copy-start.36 = (pred[12]{0:T(512)(128)(4,1)S(1)}, pred[12]{0:T(512)(128)(4,1)}, u32[]{:S(2)}) copy-start(pred[12]{0:T(512)(128)(4,1)} %eq.135) | copy-start | bytes 40
  309.0 579.0 %all-reduce.14.cloned.1.call-start = ((), (), s32[]{:S(2)}) async-start(), calls=%async_computation.2 | async-start | bytes 589824 | tf_op jit(solution)/shard_map/psum | solution.py:71
  381.1 5.2 collective-permute-start.7
  386.4 5.9 collective-permute-start.8
  392.4 9.1 collective-permute-start.9
  401.7 4.3 collective-permute-start.10
  406.6 15.4 collective-permute-start.11
  439.2 18.1 collective-permute-start.12
  445.7 11.9 collective-permute-start.13
  610.4 13.4 collective-permute-start.14
  614.8 9.0 collective-permute-start.15
  616.4 192.7 %copy-start.47 = (pred[3]{0:T(512)(128)(4,1)}, pred[3]{0:T(512)(128)(4,1)S(1)}, u32[]{:S(2)}) copy-start(pred[3]{0:T(512)(128)(4,1)S(1)} %get-tuple-element.459) | copy-start | bytes 13
  616.4 192.7 %copy-start.49 = (pred[3]{0:T(512)(128)(4,1)}, pred[3]{0:T(512)(128)(4,1)S(1)}, u32[]{:S(2)}) copy-start(pred[3]{0:T(512)(128)(4,1)S(1)} %get-tuple-element.463) | copy-start | bytes 13
  616.4 192.7 %copy-start.51 = (pred[3]{0:T(512)(128)(4,1)}, pred[3]{0:T(512)(128)(4,1)S(1)}, u32[]{:S(2)}) copy-start(pred[3]{0:T(512)(128)(4,1)S(1)} %get-tuple-element.464) | copy-start | bytes 13
  616.4 194.4 %copy-start.42 = (pred[3]{0:T(512)(128)(4,1)}, pred[3]{0:T(512)(128)(4,1)S(1)}, u32[]{:S(2)}) copy-start(pred[3]{0:T(512)(128)(4,1)S(1)} %get-tuple-element.457) | copy-start | bytes 13
  616.5 194.4 %copy-start.44 = (pred[3]{0:T(512)(128)(4,1)}, pred[3]{0:T(512)(128)(4,1)S(1)}, u32[]{:S(2)}) copy-start(pred[3]{0:T(512)(128)(4,1)S(1)} %get-tuple-element.458) | copy-start | bytes 13
  616.5 194.4 %copy-start.45 = (pred[3]{0:T(512)(128)(4,1)}, pred[3]{0:T(512)(128)(4,1)S(1)}, u32[]{:S(2)}) copy-start(pred[3]{0:T(512)(128)(4,1)S(1)} %get-tuple-element.461) | copy-start | bytes 13
  616.5 194.4 %copy-start.46 = (pred[3]{0:T(512)(128)(4,1)}, pred[3]{0:T(512)(128)(4,1)S(1)}, u32[]{:S(2)}) copy-start(pred[3]{0:T(512)(128)(4,1)S(1)} %get-tuple-element.462) | copy-start | bytes 13
  616.5 196.6 %copy-start.40 = (pred[3]{0:T(512)(128)(4,1)}, pred[3]{0:T(512)(128)(4,1)S(1)}, u32[]{:S(2)}) copy-start(pred[3]{0:T(512)(128)(4,1)S(1)} %get-tuple-element.460) | copy-start | bytes 13
  816.2 691.8 %all-reduce.16.cloned.1.call-start = ((), (), s32[]{:S(2)}) async-start(), calls=%async_computation.3 | async-start | bytes 589824 | tf_op jit(solution)/shard_map/psum | solution.py:71
  889.1 5.2 collective-permute-start.16
  894.4 5.9 collective-permute-start.17
  900.4 9.1 collective-permute-start.18
  909.8 4.3 collective-permute-start.19
  914.4 56.6 %collective-permute-start.20 = (bf16[3,4,48,512]{3,2,1,0:T(8,128)(2,1)S(1)}, bf16[3,4,48,512]{3,2,1,0:T(8,128)(2,1)S(1)}, u32[]{:S(2)}, u32[]{:S(2)}) collective-permute-start(bf16[3,4,48,512]{3,2,1,0:T(8,128)(2,1)S(1)} %concatenate.226), channel_id=1, source_target_pairs={{0,16},{1,17},{2,18},{3,19},{4,20},{5,21},{6,22},{7,23},{8,24},{9,... | collective-permute-start | bytes 1769480 | tf_op jit(solution)/shard_map/ppermute | solution.py:15
  1206.1 32.4 %collective-permute-start.21 = (bf16[3,48,1,258]{3,1,2,0:T(8,128)(2,1)S(1)}, bf16[3,48,1,258]{3,1,2,0:T(8,128)(2,1)S(1)}, u32[]{:S(2)}, u32[]{:S(2)}) collective-permute-start(bf16[3,48,1,258]{3,1,2,0:T(8,128)(2,1)S(1)} %copy.2868), channel_id=1, source_target_pairs={{0,1},{1,2},{2,3},{3,4},{4,5},{5,6},{6,7},{8,9},{9,10},{10,11},{11... | collective-permute-start | bytes 222920 | tf_op jit(solution)/shard_map/ppermute | solution.py:31
  1223.0 15.5 collective-permute-start.22
  1435.0 335.3 %all-reduce.18.cloned.1.call-start = ((), (), s32[]{:S(2)}) async-start(), calls=%async_computation.4 | async-start | bytes 884736 | tf_op jit(solution)/shard_map/psum | solution.py:231
  1509.0 7.8 collective-permute-start.23
  1517.6 47.6 %collective-permute-start.24 = (bf16[3,4,48,64]{3,2,1,0:T(8,128)(2,1)}, bf16[3,4,48,64]{3,2,1,0:T(8,128)(2,1)}, u32[]{:S(2)}, u32[]{:S(2)}) collective-permute-start(bf16[3,4,48,64]{3,2,1,0:T(8,128)(2,1)} %pad_maximum_fusion.22), channel_id=1, source_target_pairs={{0,30},{1,31},{2,0},{3,1},{4,2},{5,3},{6,4},{7,5},{8,6},{9,7},{10,... | collective-permute-start | bytes 221192 | tf_op jit(solution)/shard_map/ppermute | solution.py:15
  1566.3 29.1 %collective-permute-start.25 = (bf16[3,4,48,128]{3,2,1,0:T(8,128)(2,1)S(1)}, bf16[3,4,48,128]{3,2,1,0:T(8,128)(2,1)S(1)}, u32[]{:S(2)}, u32[]{:S(2)}) collective-permute-start(bf16[3,4,48,128]{3,2,1,0:T(8,128)(2,1)S(1)} %pad_maximum_fusion.23), channel_id=1, source_target_pairs={{0,28},{1,29},{2,30},{3,31},{4,0},{5,1},{6,2},{7,3},{8,4},{9,5},{1... | collective-permute-start | bytes 442376 | tf_op jit(solution)/shard_map/ppermute | solution.py:15
  1597.3 88.3 %collective-permute-start.26 = (bf16[3,4,48,256]{3,2,1,0:T(8,128)(2,1)}, bf16[3,4,48,256]{3,2,1,0:T(8,128)(2,1)}, u32[]{:S(2)}, u32[]{:S(2)}) collective-permute-start(bf16[3,4,48,256]{3,2,1,0:T(8,128)(2,1)} %pad_maximum_fusion.9), channel_id=1, source_target_pairs={{0,24},{1,25},{2,26},{3,27},{4,28},{5,29},{6,30},{7,31},{8,0},{9,1... | collective-permute-start | bytes 884744 | tf_op jit(solution)/shard_map/ppermute | solution.py:15
  1687.0 86.9 %collective-permute-start.27 = (bf16[3,4,48,512]{3,2,1,0:T(8,128)(2,1)S(1)}, bf16[3,4,48,512]{3,2,1,0:T(8,128)(2,1)S(1)}, u32[]{:S(2)}, u32[]{:S(2)}) collective-permute-start(bf16[3,4,48,512]{3,2,1,0:T(8,128)(2,1)S(1)} %concatenate.232), channel_id=1, source_target_pairs={{0,16},{1,17},{2,18},{3,19},{4,20},{5,21},{6,22},{7,23},{8,24},{9,... | collective-permute-start | bytes 1769480 | tf_op jit(solution)/shard_map/ppermute | solution.py:15
  (52 other events, 1918.4 us)
Sparse Core Ops, SparseCore 0:
  19.3 74.3 all-reduce.9
  309.1 70.8 all-reduce.11
  816.3 71.6 all-reduce.13
  1435.1 72.7 all-reduce.15
  1645.3 124.9 all-reduce.17
